TPU v7x, 128 devices: a whole 4x4x4 slice. The times are simulated.
128 devices in a mesh: aux: 4 (over y), tile: 32 (over x, z, core).
Axes of the slice: x: 4, y: 4, z: 4, core: 2. Of those that a mesh axis runs over, the one named last changes fastest.
Arguments:
- integrals: bfloat16 [11904, 8, 2944], P(('aux', 'tile')), may hold values from -0.57421875 to 0.57421875
- coefficients: bfloat16 [2944, 2048], replicated, may hold values from -0.109375 to 0.109375
- owned_tiles: int32 [2, 64], replicated, may hold values from 0 to 63, each once within a row
- pair_list: int32 [2, 64, 4], P(None, 'tile'), may hold values from -1 to 63, as said below
- amplitudes: bfloat16 [2, 64, 4, 128, 128], P(None, 'tile'), may hold values from -0.25 to 0.25
Outputs:
- residual: float32 [2, 64, 128, 128], P(None, 'tile')
Inputs may be any that keep to these rules, and one draw needn't show every extreme that they name: `pair_list`: every live entry of slot s is a slot within 2 of s; the live entries of one slot are distinct; -1 marks an entry dropped by screening.
All inputs are finite; a program needn't handle non-finite values.
Results may differ from a plain program's by a relative error of at most 0.00087.
Values may be sent and summed in bfloat16 or wider, within the bound.
A program may use at most 128 MiB of HBM per device.

v0:
```python
import jax
import jax.numpy as jnp
from jax import lax
from jax.sharding import PartitionSpec as P

NB = 2


def per_device(integrals, coefficients, owned_tiles, pair_list, amplitudes):
    tile_count = lax.axis_size("tile")
    q_rows, occ_all, ao_count = integrals.shape
    virt_count = coefficients.shape[1]
    tile_width = amplitudes.shape[-1]
    virt_tiles = virt_count // tile_width
    per_dev = pair_list.shape[1]
    occ_batch = occ_all // NB
    total_slots = owned_tiles.shape[1]
    first_slot = lax.axis_index("tile") * per_dev
    positions = jnp.arange(3 * per_dev, dtype=jnp.int32)
    results = []
    for occ_group in range(NB):
        int_block = integrals[:, occ_group * occ_batch : (occ_group + 1) * occ_batch, :].reshape(
            q_rows * occ_batch, ao_count
        )
        half_done = jnp.dot(int_block, coefficients, preferred_element_type=jnp.float32).astype(
            jnp.bfloat16
        )
        half_done = half_done.reshape(q_rows, occ_batch * virt_tiles, tile_width)
        ordered = jnp.take(half_done, owned_tiles[occ_group], axis=1)
        zero_pad = jnp.zeros((q_rows, per_dev, tile_width), jnp.bfloat16)
        padded = jnp.concatenate([zero_pad, ordered, zero_pad], axis=1)
        below_part = padded[:, :total_slots].reshape(q_rows, tile_count, per_dev, tile_width)
        middle = ordered.reshape(q_rows, tile_count, per_dev, tile_width)
        above_part = padded[:, 2 * per_dev :].reshape(q_rows, tile_count, per_dev, tile_width)
        bundle = jnp.concatenate([below_part, middle, above_part], axis=2)
        arrived = lax.all_to_all(bundle, "tile", split_axis=1, concat_axis=0, tiled=True)
        extended = arrived.reshape(q_rows * tile_count, 3 * per_dev, tile_width)
        mine = extended[:, per_dev : 2 * per_dev]
        listed = pair_list[occ_group]
        ext_place = listed - (first_slot - per_dev)
        selector = (
            (ext_place[:, :, None] == positions[None, None, :]) & (listed[:, :, None] >= 0)
        ).astype(jnp.float32)
        amp_tiles = amplitudes[occ_group]
        cross_ints = jnp.einsum("qja,qeb->jeab", mine, extended, preferred_element_type=jnp.float32)
        partial_value = jnp.einsum(
            "jke,jeab->jkab", selector, cross_ints, precision=lax.Precision.HIGHEST
        )
        summed = lax.psum(partial_value, "aux")
        residue = jnp.einsum(
            "jkab,jkbc->jac", summed, amp_tiles.astype(jnp.float32), precision=lax.Precision.HIGHEST
        )
        results.append(residue)
    return jnp.stack(results)


def solution(mesh):
    in_specs = (
        P(("aux", "tile"), None, None),
        P(),
        P(),
        P(None, "tile", None),
        P(None, "tile", None, None, None),
    )
    out_specs = P(None, "tile", None, None)
    return jax.shard_map(
        per_device, mesh=mesh, in_specs=in_specs, out_specs=out_specs, check_vma=False
    )
```

profile of v0, /device:TPU:0, one launch (start us, length us, event | category | flops | bytes accessed | tf_op | source)
XLA Modules:
  0.0 286.1 jit_solution(10070424365951236372)
XLA Ops:
  7.3 6.6 %fusion.28 = (bf16[93,4,2944]{2,1,0:T(4,128)(2,1)}, bf16[93,4,2944]{2,1,0:T(4,128)(2,1)S(1)}) fusion(bf16[93,8,2944]{2,1,0:T(8,128)(2,1)} %param.7), kind=kLoop, calls=%fused_computation.51 | loop fusion | bytes 8761344 | tf_op jit(solution)/shard_map/slice | solution.py:22
  13.9 4.4 %reshape.75 = bf16[372,2944]{1,0:T(8,128)(2,1)} reshape(bf16[93,4,2944]{2,1,0:T(4,128)(2,1)} %get-tuple-element.12) | data formatting | bytes 4380672 | tf_op jit(solution)/shard_map/reshape | solution.py:22
  18.3 11.2 %convolution_convert_fusion.1 = bf16[372,2048]{1,0:T(8,128)(2,1)} fusion(bf16[372,2944]{1,0:T(8,128)(2,1)} %reshape.75, bf16[2944,2048]{1,0:T(8,128)(2,1)} %param.8), kind=kOutput, calls=%fused_computation.9 | convolution fusion | flops 4486569984 | bytes 15772672 | tf_op jit(solution)/shard_map/dot_general | solution.py:25
  29.5 3.7 %reshape.76 = bf16[93,64,128]{2,1,0:T(8,128)(2,1)} reshape(bf16[372,2048]{1,0:T(8,128)(2,1)} %convolution_convert_fusion.1) | data formatting | bytes 3047424 | tf_op jit(solution)/shard_map/reshape | solution.py:28
  33.2 3.6 %copy.14 = bf16[93,64,128]{2,0,1:T(8,128)(2,1)} copy(bf16[93,64,128]{2,1,0:T(8,128)(2,1)} %reshape.76) | data formatting | bytes 3047424 | tf_op jit(solution)/shard_map/reshape | solution.py:28
  36.8 2.6 reshape.81
  39.4 10.0 %convolution_convert_fusion = bf16[372,2048]{1,0:T(8,128)(2,1)S(1)} fusion(bf16[372,2944]{1,0:T(8,128)(2,1)} %reshape.81, bf16[2944,2048]{1,0:T(8,128)(2,1)} %param.8), kind=kOutput, calls=%fused_computation.8 | convolution fusion | flops 4486569984 | bytes 15772672 | tf_op jit(solution)/shard_map/dot_general | solution.py:25
  51.3 2.5 copy.18
  57.6 2.2 broadcast_select_fusion
  60.3 2.5 pad_maximum_fusion
  62.7 8.4 %all-to-all-start = ((bf16[93,32,6,128]{3,0,2,1:T(8,128)(2,1)}), bf16[93,32,6,128]{3,0,2,1:T(8,128)(2,1)}, u32[]{:S(2)}, u32[]{:S(2)}) async-start(bf16[93,32,6,128]{3,0,2,1:T(8,128)(2,1)} %pad_maximum_fusion), calls=%async_computation | async-start | bytes 9437184 | tf_op jit(solution)/shard_map/all_to_all | solution.py:36
  71.5 2.4 pad_maximum_fusion.1
  73.9 56.1 %all-to-all-done = bf16[93,32,6,128]{3,0,2,1:T(8,128)(2,1)} async-done(((bf16[93,32,6,128]{3,0,2,1:T(8,128)(2,1)}), bf16[93,32,6,128]{3,0,2,1:T(8,128)(2,1)}, u32[]{:S(2)}, u32[]{:S(2)}) %all-to-all-start) | async-done | bytes 4571168 | tf_op jit(solution)/shard_map/all_to_all | solution.py:36
  130.0 7.2 %all-to-all-start.1 = ((bf16[93,32,6,128]{3,0,2,1:T(8,128)(2,1)}), bf16[93,32,6,128]{3,0,2,1:T(8,128)(2,1)}, u32[]{:S(2)}, u32[]{:S(2)}) async-start(bf16[93,32,6,128]{3,0,2,1:T(8,128)(2,1)} %pad_maximum_fusion.1), calls=%async_computation.1 | async-start | bytes 9437184 | tf_op jit(solution)/shard_map/all_to_all | solution.py:36
  137.4 5.5 %copy.15 = bf16[32,93,1,6,128]{4,1,0,3,2:T(8,128)(2,1)} copy(bf16[32,93,1,6,128]{4,1,3,0,2:T(8,128)(2,1)} %bitcast.10) | data formatting | bytes 9142272 | tf_op jit(solution)/shard_map/all_to_all | solution.py:36
  142.9 7.4 %reshape.109 = bf16[2976,6,128,1]{2,0,1,3:T(8,128)(2,1)} reshape(bf16[32,93,1,6,128]{4,1,0,3,2:T(8,128)(2,1)} %copy.15) | data formatting | bytes 9142272 | tf_op jit(solution)/shard_map/reshape | solution.py:37
  150.3 7.3 %reshape.80 = bf16[2976,6,128]{2,0,1:T(8,128)(2,1)} reshape(bf16[32,93,1,6,128]{4,1,0,3,2:T(8,128)(2,1)} %copy.15) | data formatting | bytes 9142272 | tf_op jit(solution)/shard_map/reshape | solution.py:37
  157.6 38.8 %all-to-all-done.1 = bf16[93,32,6,128]{3,0,2,1:T(8,128)(2,1)} async-done(((bf16[93,32,6,128]{3,0,2,1:T(8,128)(2,1)}), bf16[93,32,6,128]{3,0,2,1:T(8,128)(2,1)}, u32[]{:S(2)}, u32[]{:S(2)}) %all-to-all-start.1) | async-done | bytes 4571168 | tf_op jit(solution)/shard_map/all_to_all | solution.py:36
  196.4 5.5 %copy.19 = bf16[32,93,1,6,128]{4,1,0,3,2:T(8,128)(2,1)} copy(bf16[32,93,1,6,128]{4,1,3,0,2:T(8,128)(2,1)} %bitcast.28) | data formatting | bytes 9142272 | tf_op jit(solution)/shard_map/all_to_all | solution.py:36
  201.9 7.4 %reshape.113 = bf16[2976,6,128,1]{2,0,1,3:T(8,128)(2,1)} reshape(bf16[32,93,1,6,128]{4,1,0,3,2:T(8,128)(2,1)} %copy.19) | data formatting | bytes 9142272 | tf_op jit(solution)/shard_map/reshape | solution.py:37
  209.3 7.4 %reshape.86 = bf16[2976,6,128]{2,0,1:T(8,128)(2,1)} reshape(bf16[32,93,1,6,128]{4,1,0,3,2:T(8,128)(2,1)} %copy.19) | data formatting | bytes 9142272 | tf_op jit(solution)/shard_map/reshape | solution.py:37
  216.6 4.2 %fusion.4 = f32[2,6,128,128]{2,3,0,1:T(8,128)S(1)} fusion(bf16[2976,6,128]{2,0,1:T(8,128)(2,1)} %reshape.80, bf16[2976,6,128,1]{2,0,1,3:T(8,128)(2,1)} %reshape.109), kind=kOutput, calls=%fused_computation.18 | convolution fusion | flops 1170210816 | bytes 6881280 | tf_op jit(solution)/shard_map/qja,qeb->jeab/dot_general | solution.py:45
  221.3 4.2 %fusion.7 = f32[2,6,128,128]{2,3,0,1:T(8,128)S(1)} fusion(bf16[2976,6,128]{2,0,1:T(8,128)(2,1)} %reshape.86, bf16[2976,6,128,1]{2,0,1,3:T(8,128)(2,1)} %reshape.113), kind=kOutput, calls=%fused_computation.19 | convolution fusion | flops 1170210816 | bytes 6881280 | tf_op jit(solution)/shard_map/qja,qeb->jeab/dot_general | solution.py:45
  228.8 46.9 %all-reduce.7.cloned.1.call-done = (f32[2,4,128,128]{3,1,2,0:T(4,128)}, f32[2,4,128,128]{3,1,2,0:T(4,128)}) async-done(((f32[2,4,128,128]{3,1,2,0:T(4,128)}, f32[2,4,128,128]{3,1,2,0:T(4,128)}), (f32[2,4,128,128]{3,1,2,0:T(4,128)}, f32[2,4,128,128]{3,1,2,0:T(4,128)})) %all-reduce.7.cloned.1.call-update) | async-done | bytes 1048592 | tf_op jit(solution)/shard_map/psum | solution.py:49
  (25 shorter events, 14.6 us)
Async XLA Ops:
  51.3 2.5 copy-start
  62.7 67.3 %all-to-all-start = ((bf16[93,32,6,128]{3,0,2,1:T(8,128)(2,1)}), bf16[93,32,6,128]{3,0,2,1:T(8,128)(2,1)}, u32[]{:S(2)}, u32[]{:S(2)}) async-start(bf16[93,32,6,128]{3,0,2,1:T(8,128)(2,1)} %pad_maximum_fusion), calls=%async_computation | async-start | bytes 9437184 | tf_op jit(solution)/shard_map/all_to_all | solution.py:36
  73.9 63.4 %copy-start.2 = (s32[2,2,4]{2,1,0:T(2,128)S(1)}, s32[2,2,4]{2,1,0:T(2,128)}, u32[]{:S(2)}) copy-start(s32[2,2,4]{2,1,0:T(2,128)} %param.10) | copy-start | bytes 196
  130.0 66.4 %all-to-all-start.1 = ((bf16[93,32,6,128]{3,0,2,1:T(8,128)(2,1)}), bf16[93,32,6,128]{3,0,2,1:T(8,128)(2,1)}, u32[]{:S(2)}, u32[]{:S(2)}) async-start(bf16[93,32,6,128]{3,0,2,1:T(8,128)(2,1)} %pad_maximum_fusion.1), calls=%async_computation.1 | async-start | bytes 9437184 | tf_op jit(solution)/shard_map/all_to_all | solution.py:36
  137.3 138.4 %all-reduce.7.cloned.1.call-start = ((), (), s32[]{:S(2)}) async-start(), calls=%async_computation.2 | async-start | bytes 2097152 | tf_op jit(solution)/shard_map/psum | solution.py:49
  225.9 49.8 %copy-start.1 = (bf16[2,2,4,128,128]{4,3,2,1,0:T(8,128)(2,1)S(1)}, bf16[2,2,4,128,128]{4,3,2,1,0:T(8,128)(2,1)}, u32[]{:S(2)}) copy-start(bf16[2,2,4,128,128]{4,3,2,1,0:T(8,128)(2,1)} %param.11) | copy-start | bytes 1572868
Sparse Core Ops, SparseCore 0:
  228.9 46.7 all-reduce.6
where the time goes:
time: 287 us; the launch traced here: 286 us
  waiting for transfers between devices  142 us (49%)
  local copies, waits for them, and re-layouts  71.2 us (25%)
  matrix products  35.3 us (12%)
  starting transfers between devices  15.6 us (5%)
  between operations  13.5 us (5%)
  other arithmetic  8.62 us (3%)
    all_to_all x2, waiting for transfers between devices, per_device(): lax.all_to_all(bundle, 'tile', split_axis=1, concat_axis=0, tiled=True)  94.9 us
    psum x1, waiting for transfers between devices, per_device(): summed = lax.psum(partial_value, 'aux')  46.9 us
    reshape x4, local copies, waits for them, and re-layouts, per_device(): extended = arrived.reshape(q_rows * tile_count, 3 * per_dev, tile_width)  29.5 us
    dot_general x2, matrix products, per_device(): jnp.dot(int_block, coefficients, preferred_element_type=jnp.float32)  21.2 us
    all_to_all x2, starting transfers between devices, per_device(): lax.all_to_all(bundle, 'tile', split_axis=1, concat_axis=0, tiled=True)  15.6 us
    reshape x4, local copies, waits for them, and re-layouts, per_device(): half_done = half_done.reshape(q_rows, occ_batch * virt_tiles, tile_width)  11.6 us
    all_to_all x2, local copies, waits for them, and re-layouts, per_device(): lax.all_to_all(bundle, 'tile', split_axis=1, concat_axis=0, tiled=True)  11 us
    dot_general x2, matrix products, per_device(): jnp.einsum('qja,qeb->jeab', mine, extended, preferred_element_type=jnp.fl...  8.4 us
  transfers between devices with their start and end apart: 3, of which 3 were waited for; matrix products, arithmetic and copies ran while one was open for 8% of the time, Pallas kernels for 0%

commit v1 on v0

--- a/solution.py
+++ b/solution.py
@@ -46,7 +46,7 @@
         partial_value = jnp.einsum(
             "jke,jeab->jkab", selector, cross_ints, precision=lax.Precision.HIGHEST
         )
-        summed = lax.psum(partial_value, "aux")
+        summed = jnp.sum(lax.all_gather(partial_value, "aux"), axis=0)
         residue = jnp.einsum(
             "jkab,jkbc->jac", summed, amp_tiles.astype(jnp.float32), precision=lax.Precision.HIGHEST
         )

time: 287 us -> 267 us (0.930)
  waiting for transfers between devices: 142 us -> 119 us
  matrix products: 35.3 us -> 31.6 us
  other arithmetic: 8.62 us -> 12.2 us
    psum x1 -> x0, waiting for transfers between devices: 46.9 us -> none  [per_device(): summed = lax.psum(partial_value, 'aux')]
    all_gather x0 -> x2, waiting for transfers between devices: none -> 30.1 us  [per_device(): summed = jnp.sum(lax.all_gather(partial_value, 'aux'), axis=0)]
    all_to_all x2, waiting for transfers between devices: 94.9 us -> 88.9 us  [per_device(): lax.all_to_all(bundle, 'tile', split_axis=1, concat_axis=0, tiled=True)]
    reduce_sum x0 -> x2, other arithmetic: none -> 3.57 us  [per_device(): summed = jnp.sum(lax.all_gather(partial_value, 'aux'), axis=0)]
  transfers between devices with their start and end apart: 3 -> 4, of which waited for: 3 -> 3; matrix products, arithmetic and copies ran while one was open for 8% -> 22% of each run, Pallas kernels for 0% -> 0%
where the time goes in v1:
time: 267 us; the launch traced here: 265 us
  waiting for transfers between devices  119 us (45%)
  local copies, waits for them, and re-layouts  72.6 us (27%)
  matrix products  31.6 us (12%)
  starting transfers between devices  15.7 us (6%)
  between operations  13.6 us (5%)
  other arithmetic  12.2 us (5%)
    all_to_all x2, waiting for transfers between devices, per_device(): lax.all_to_all(bundle, 'tile', split_axis=1, concat_axis=0, tiled=True)  88.9 us
    all_gather x2, waiting for transfers between devices, per_device(): summed = jnp.sum(lax.all_gather(partial_value, 'aux'), axis=0)  30.1 us
    reshape x4, local copies, waits for them, and re-layouts, per_device(): extended = arrived.reshape(q_rows * tile_count, 3 * per_dev, tile_width)  29.3 us
    dot_general x2, matrix products, per_device(): jnp.dot(int_block, coefficients, preferred_element_type=jnp.float32)  21.2 us
    all_to_all x2, starting transfers between devices, per_device(): lax.all_to_all(bundle, 'tile', split_axis=1, concat_axis=0, tiled=True)  15.6 us
    reshape x4, local copies, waits for them, and re-layouts, per_device(): half_done = half_done.reshape(q_rows, occ_batch * virt_tiles, tile_width)  11.6 us
    all_to_all x2, local copies, waits for them, and re-layouts, per_device(): lax.all_to_all(bundle, 'tile', split_axis=1, concat_axis=0, tiled=True)  10.9 us
    dot_general x2, matrix products, per_device(): jnp.einsum('qja,qeb->jeab', mine, extended, preferred_element_type=jnp.fl...  8.39 us
  transfers between devices with their start and end apart: 4, of which 3 were waited for; matrix products, arithmetic and copies ran while one was open for 22% of the time, Pallas kernels for 0%

profile of v1, /device:TPU:0, one launch (start us, length us, event | category | flops | bytes accessed | tf_op | source)
XLA Modules:
  0.0 264.6 jit_solution(15112325244490030799)
XLA Ops:
  7.3 6.6 %fusion.26 = (bf16[93,4,2944]{2,1,0:T(4,128)(2,1)}, bf16[93,4,2944]{2,1,0:T(4,128)(2,1)S(1)}) fusion(bf16[93,8,2944]{2,1,0:T(8,128)(2,1)} %param.7), kind=kLoop, calls=%fused_computation.49 | loop fusion | bytes 8761344 | tf_op jit(solution)/shard_map/slice | solution.py:22
  13.9 4.4 %reshape.75 = bf16[372,2944]{1,0:T(8,128)(2,1)} reshape(bf16[93,4,2944]{2,1,0:T(4,128)(2,1)} %get-tuple-element.10) | data formatting | bytes 4380672 | tf_op jit(solution)/shard_map/reshape | solution.py:22
  18.3 11.2 %convolution_convert_fusion.1 = bf16[372,2048]{1,0:T(8,128)(2,1)} fusion(bf16[372,2944]{1,0:T(8,128)(2,1)} %reshape.75, bf16[2944,2048]{1,0:T(8,128)(2,1)} %param.8), kind=kOutput, calls=%fused_computation.9 | convolution fusion | flops 4486569984 | bytes 15772672 | tf_op jit(solution)/shard_map/dot_general | solution.py:25
  29.5 3.7 %reshape.76 = bf16[93,64,128]{2,1,0:T(8,128)(2,1)} reshape(bf16[372,2048]{1,0:T(8,128)(2,1)} %convolution_convert_fusion.1) | data formatting | bytes 3047424 | tf_op jit(solution)/shard_map/reshape | solution.py:28
  33.2 3.5 %copy.14 = bf16[93,64,128]{2,0,1:T(8,128)(2,1)} copy(bf16[93,64,128]{2,1,0:T(8,128)(2,1)} %reshape.76) | data formatting | bytes 3047424 | tf_op jit(solution)/shard_map/reshape | solution.py:28
  36.7 2.6 reshape.81
  39.4 10.0 %convolution_convert_fusion = bf16[372,2048]{1,0:T(8,128)(2,1)S(1)} fusion(bf16[372,2944]{1,0:T(8,128)(2,1)} %reshape.81, bf16[2944,2048]{1,0:T(8,128)(2,1)} %param.8), kind=kOutput, calls=%fused_computation.8 | convolution fusion | flops 4486569984 | bytes 15772672 | tf_op jit(solution)/shard_map/dot_general | solution.py:25
  51.3 2.5 copy.20
  57.6 2.2 broadcast_select_fusion
  60.2 2.4 pad_maximum_fusion
  62.7 8.4 %all-to-all-start = ((bf16[93,32,6,128]{3,0,2,1:T(8,128)(2,1)}), bf16[93,32,6,128]{3,0,2,1:T(8,128)(2,1)}, u32[]{:S(2)}, u32[]{:S(2)}) async-start(bf16[93,32,6,128]{3,0,2,1:T(8,128)(2,1)} %pad_maximum_fusion), calls=%async_computation | async-start | bytes 9437184 | tf_op jit(solution)/shard_map/all_to_all | solution.py:36
  71.4 2.5 pad_maximum_fusion.1
  73.9 56.1 %all-to-all-done = bf16[93,32,6,128]{3,0,2,1:T(8,128)(2,1)} async-done(((bf16[93,32,6,128]{3,0,2,1:T(8,128)(2,1)}), bf16[93,32,6,128]{3,0,2,1:T(8,128)(2,1)}, u32[]{:S(2)}, u32[]{:S(2)}) %all-to-all-start) | async-done | bytes 4571168 | tf_op jit(solution)/shard_map/all_to_all | solution.py:36
  130.0 7.2 %all-to-all-start.1 = ((bf16[93,32,6,128]{3,0,2,1:T(8,128)(2,1)}), bf16[93,32,6,128]{3,0,2,1:T(8,128)(2,1)}, u32[]{:S(2)}, u32[]{:S(2)}) async-start(bf16[93,32,6,128]{3,0,2,1:T(8,128)(2,1)} %pad_maximum_fusion.1), calls=%async_computation.1 | async-start | bytes 9437184 | tf_op jit(solution)/shard_map/all_to_all | solution.py:36
  137.3 5.4 %copy.15 = bf16[32,93,1,6,128]{4,1,0,3,2:T(8,128)(2,1)} copy(bf16[32,93,1,6,128]{4,1,3,0,2:T(8,128)(2,1)} %bitcast.10) | data formatting | bytes 9142272 | tf_op jit(solution)/shard_map/all_to_all | solution.py:36
  142.8 7.3 %reshape.111 = bf16[2976,6,128,1]{2,0,1,3:T(8,128)(2,1)} reshape(bf16[32,93,1,6,128]{4,1,0,3,2:T(8,128)(2,1)} %copy.15) | data formatting | bytes 9142272 | tf_op jit(solution)/shard_map/reshape | solution.py:37
  150.1 7.3 %reshape.80 = bf16[2976,6,128]{2,0,1:T(8,128)(2,1)} reshape(bf16[32,93,1,6,128]{4,1,0,3,2:T(8,128)(2,1)} %copy.15) | data formatting | bytes 9142272 | tf_op jit(solution)/shard_map/reshape | solution.py:37
  157.4 4.2 %fusion.4 = f32[2,6,128,128]{2,3,0,1:T(8,128)S(1)} fusion(bf16[2976,6,128]{2,0,1:T(8,128)(2,1)} %reshape.80, bf16[2976,6,128,1]{2,0,1,3:T(8,128)(2,1)} %reshape.111), kind=kOutput, calls=%fused_computation.18 | convolution fusion | flops 1170210816 | bytes 6881280 | tf_op jit(solution)/shard_map/qja,qeb->jeab/dot_general | solution.py:45
  163.6 32.8 %all-to-all-done.1 = bf16[93,32,6,128]{3,0,2,1:T(8,128)(2,1)} async-done(((bf16[93,32,6,128]{3,0,2,1:T(8,128)(2,1)}), bf16[93,32,6,128]{3,0,2,1:T(8,128)(2,1)}, u32[]{:S(2)}, u32[]{:S(2)}) %all-to-all-start.1) | async-done | bytes 4571168 | tf_op jit(solution)/shard_map/all_to_all | solution.py:36
  196.4 5.5 %copy.21 = bf16[32,93,1,6,128]{4,1,0,3,2:T(8,128)(2,1)} copy(bf16[32,93,1,6,128]{4,1,3,0,2:T(8,128)(2,1)} %bitcast.29) | data formatting | bytes 9142272 | tf_op jit(solution)/shard_map/all_to_all | solution.py:36
  201.9 7.3 %reshape.115 = bf16[2976,6,128,1]{2,0,1,3:T(8,128)(2,1)} reshape(bf16[32,93,1,6,128]{4,1,0,3,2:T(8,128)(2,1)} %copy.21) | data formatting | bytes 9142272 | tf_op jit(solution)/shard_map/reshape | solution.py:37
  209.2 7.3 %reshape.86 = bf16[2976,6,128]{2,0,1:T(8,128)(2,1)} reshape(bf16[32,93,1,6,128]{4,1,0,3,2:T(8,128)(2,1)} %copy.21) | data formatting | bytes 9142272 | tf_op jit(solution)/shard_map/reshape | solution.py:37
  216.5 4.2 %fusion.7 = f32[2,6,128,128]{2,3,0,1:T(8,128)S(1)} fusion(bf16[2976,6,128]{2,0,1:T(8,128)(2,1)} %reshape.86, bf16[2976,6,128,1]{2,0,1,3:T(8,128)(2,1)} %reshape.115), kind=kOutput, calls=%fused_computation.19 | convolution fusion | flops 1170210816 | bytes 6881280 | tf_op jit(solution)/shard_map/qja,qeb->jeab/dot_general | solution.py:45
  224.5 30.1 %all-gather.7.cloned.1.call-done = f32[8,4,128,128]{3,2,1,0:T(8,128)} async-done(((f32[2,4,128,128]{3,2,1,0:T(8,128)}), f32[8,4,128,128]{3,2,1,0:T(8,128)}) %all-gather.7.cloned.1.call-update) | async-done | bytes 2097168 | tf_op jit(solution)/shard_map/all_gather | solution.py:49
  (32 shorter events, 16.2 us)
Async XLA Ops:
  51.3 2.5 copy-start
  62.7 67.3 %all-to-all-start = ((bf16[93,32,6,128]{3,0,2,1:T(8,128)(2,1)}), bf16[93,32,6,128]{3,0,2,1:T(8,128)(2,1)}, u32[]{:S(2)}, u32[]{:S(2)}) async-start(bf16[93,32,6,128]{3,0,2,1:T(8,128)(2,1)} %pad_maximum_fusion), calls=%async_computation | async-start | bytes 9437184 | tf_op jit(solution)/shard_map/all_to_all | solution.py:36
  73.9 63.4 %copy-start.2 = (s32[2,2,4]{2,1,0:T(2,128)S(1)}, s32[2,2,4]{2,1,0:T(2,128)}, u32[]{:S(2)}) copy-start(s32[2,2,4]{2,1,0:T(2,128)} %param.10) | copy-start | bytes 196
  130.0 66.4 %all-to-all-start.1 = ((bf16[93,32,6,128]{3,0,2,1:T(8,128)(2,1)}), bf16[93,32,6,128]{3,0,2,1:T(8,128)(2,1)}, u32[]{:S(2)}, u32[]{:S(2)}) async-start(bf16[93,32,6,128]{3,0,2,1:T(8,128)(2,1)} %pad_maximum_fusion.1), calls=%async_computation.1 | async-start | bytes 9437184 | tf_op jit(solution)/shard_map/all_to_all | solution.py:36
  137.2 85.4 %all-gather.5.cloned.1.call-start = ((), (), s32[]{:S(2)}) async-start(), calls=%async_computation.2 | async-start | bytes 2621440 | tf_op jit(solution)/shard_map/all_gather | solution.py:49
  163.5 91.0 %all-gather.7.cloned.1.call-start = ((), (), s32[]{:S(2)}) async-start(), calls=%async_computation.3 | async-start | bytes 2621440 | tf_op jit(solution)/shard_map/all_gather | solution.py:49
  222.6 33.7 %copy-start.1 = (bf16[2,2,4,128,128]{4,3,2,1,0:T(8,128)(2,1)S(1)}, bf16[2,2,4,128,128]{4,3,2,1,0:T(8,128)(2,1)}, u32[]{:S(2)}) copy-start(bf16[2,2,4,128,128]{4,3,2,1,0:T(8,128)(2,1)} %param.11) | copy-start | bytes 1572868
Sparse Core Ops, SparseCore 0:
  163.6 32.3 all-gather.4
  222.7 31.7 all-gather.6
